TPU v7x, 768 devices: a whole 4x8x12 slice. The times are simulated.
768 devices in a mesh: tile: 96 (over z_lo, x, y), section: 8 (over z_hi, core).
Axes of the slice: x: 4, y: 8, z: 12 (z_hi: 4, z_lo: 3; z = z_hi * 3 + z_lo), core: 2. Of those that a mesh axis runs over, the one named last changes fastest.
Arguments:
- state: float32 [5, 2, 2304, 3072], P(None, None, 'tile', 'section'), may hold values from -6 to 6
- courant: float32 [2, 2, 2304, 3072], P(None, None, 'tile', 'section'), may hold values from -0.4 to 0.4
- nest_offset: int32 [1], replicated, may hold values from 24 to 359
Outputs:
- new_state: float32 [5, 2, 2304, 3072], P(None, None, 'tile', 'section')
All inputs are finite; a program needn't handle non-finite values.
Results may differ from a plain program's by a relative error of at most 0.000053.
Values sent between devices are 32-bit elements; how exact they have to be, the bound alone decides.
A program may use at most 64 MiB of HBM per device.

v0:
```python
import functools

import jax
import jax.numpy as jnp
from jax import lax
from jax.experimental import pallas as pl
from jax.experimental.pallas import tpu as pltpu
from jax.sharding import PartitionSpec as P

RATIO = 3
ZONE = 5
DIFFUSION = 0.02
MIXING = 0.05
FIELDS = 5
LEVELS = 2
ROWS = 24
COLS = 384
LANES = 128
COARSE = ROWS // RATIO
TALL = 32
WIDE = 512
PAIRS = FIELDS * LEVELS
PLANES = FIELDS + 2
MESH = pl.DeviceIdType.MESH

NEAR = ((-1, 0), (1, 0), (0, -1), (-1, -1), (1, -1), (0, 1), (-1, 1), (1, 1))


def iota(shape, dim):
    return lax.broadcasted_iota(jnp.int32, shape, dim)


def pick(flag, one, other):
    return jnp.where(flag, one, other)


def thirds(value):
    high = value.astype(jnp.bfloat16)
    rest = value - high.astype(jnp.float32)
    middle = rest.astype(jnp.bfloat16)
    low = (rest - middle.astype(jnp.float32)).astype(jnp.bfloat16)
    return [high, middle, low]


def dot_ones(value, ones):
    rows = value.shape[0]
    parts = jnp.dot(jnp.concatenate(thirds(value), axis=0), ones, preferred_element_type=jnp.float32)
    return parts[:rows] + parts[rows : 2 * rows] + parts[2 * rows :]


def kernel(
    q, tiles, sections,
    offset_ref, state_in, courant_in, out,
    state, courant, strips, near_strips, slabs, near_slabs, side_columns,
    edge_in, spread, stage, stage_side, window_in, window_side, coef, mixed, force, slope, work,
    fine, means, relay_in, relay_out, mean_in,
    load_sem, near_send, near_recv, edge_send, edge_recv, window_send, window_recv,
    relay_send, relay_recv, mean_send, mean_recv,
):
    tile = lax.axis_index("tile")
    section = lax.axis_index("section")
    groups = tiles // RATIO
    is_parent = section < 2
    is_nest = section >= 2
    nest = section - 2
    group = tile // RATIO
    inner = tile - group * RATIO
    rest = offset_ref[0] - q * ROWS
    rim_column = (section == 2) | (section == sections - 1)
    at_top = tile == 0
    rim_row = is_nest & (at_top | (tile == tiles - 1))
    low_window = is_parent & (tile >= q - 1) & (tile <= q + 1)
    high_window = is_parent & (tile >= q + groups - 1) & (tile <= q + groups)
    in_window = low_window | high_window
    under = is_parent & (tile >= q) & (tile <= q + groups)

    def relay_tile(a):
        return lax.min(a, groups - 1) * RATIO // groups * groups + lax.rem(q + a, groups)

    turn = lax.rem(tile - q + tiles, groups)
    wrapped = (turn == 0) & (tile // groups == RATIO - 1)
    task = pick(wrapped, groups, turn)
    is_relay = is_nest & (relay_tile(task) == tile)

    def near_peer(step):
        return (
            lax.rem(tile + step[0] + tiles, tiles),
            lax.rem(section + step[1] + sections, sections),
        )

    loads = [
        pltpu.make_async_copy(state_in, state, load_sem.at[0]),
        pltpu.make_async_copy(courant_in, courant, load_sem.at[1]),
    ]
    for load in loads:
        load.start()

    @pl.when(rim_row)
    def _():
        @pl.loop(0, 3)
        def _(u):
            window_in[u] = jnp.zeros((PLANES, 8, LANES), jnp.float32)
            window_side[u] = jnp.zeros((2, 8, LANES), jnp.float32)

    barrier = pltpu.get_barrier_semaphore()

    def greet(tile_to, section_to):
        pl.semaphore_signal(
            barrier, inc=1, device_id=(tile_to, section_to), device_id_type=MESH
        )

    @pl.when(rim_column)
    def _():
        @pl.loop(0, 4)
        def _(d):
            greet(q + group + d - 1, pick(section == 2, 0, 1))

    @pl.when(rim_row)
    def _():
        @pl.loop(0, pick(at_top, 3, 2))
        def _(u):
            sender = pick(at_top, q - 1, q + groups - 1) + u

            @pl.when(nest <= 3)
            def _():
                greet(sender, 0)

            @pl.when(nest >= 2)
            def _():
                greet(sender, 1)

    for step in NEAR:
        greet(*near_peer(step))

    def relay_source(late):
        return (task - late >= 0) & (task - late < groups)

    @pl.when(is_relay)
    def _():
        @pl.loop(0, 2)
        def _(late):
            @pl.when(relay_source(late))
            def _():
                @pl.loop(0, RATIO)
                def _(b):
                    source = (task - late) * RATIO + b

                    @pl.when(source != tile)
                    def _():
                        greet(source, section)

    @pl.when(under)
    def _():
        @pl.loop(0, RATIO)
        def _(third):
            greet(relay_tile(tile - q), 2 + RATIO * section + third)

    @pl.loop(0, PAIRS)
    def _(pair):
        force[pair] = jnp.zeros((TALL, WIDE), jnp.float32)
        slope[pair] = jnp.zeros((TALL, WIDE), jnp.float32)

    for load in loads:
        load.wait()

    upper = iota((8, COLS), 0) < 4

    def pack_rows(plane, first, second):
        slabs[0, plane] = jnp.where(upper, first[0:8, :], pltpu.roll(second[0:8, :], 4, 0))
        slabs[1, plane] = jnp.where(upper, pltpu.roll(first[16:24, :], 4, 0), second[16:24, :])

    @pl.loop(0, FIELDS)
    def _(f):
        pack_rows(f, state[f, 0], state[f, 1])

    @pl.loop(0, 2)
    def _(d):
        pack_rows(FIELDS + d, courant[d, 0], courant[d, 1])

    lane = iota((ROWS, LANES), 1)

    def pack_columns(f, packed):
        left, right = packed
        for l in range(LEVELS):
            for kind in range(3):
                g = PAIRS * kind + LEVELS * f + l
                source = state.at[f, l] if kind == 0 else courant.at[kind - 1, l]
                here = (lane >= 3 * g) & (lane < 3 * g + 3)
                left = jnp.where(here, pltpu.roll(source[:, :LANES], 3 * g, 1), left)
                right = jnp.where(here, pltpu.roll(source[:, COLS - LANES :], 3 * g + 3, 1), right)
        return left, right

    blank = jnp.zeros((ROWS, LANES), jnp.float32)
    left, right = lax.fori_loop(0, FIELDS, pack_columns, (blank, blank))
    strips[0] = left
    strips[1] = right

    @pl.when(in_window)
    def _():
        start = rest + pick(low_window, -1 - ROWS * (tile - q), 21 - ROWS * (tile - q - groups + 1))
        sub = iota((8, COLS), 0)

        def window_rows(plane, source):
            value = jnp.zeros((8, COLS), jnp.float32)
            for l in range(LEVELS):
                for j in range(4):
                    row = start + j
                    owned = (row >= 0) & (row < ROWS)
                    line = source(l)[pl.ds(jnp.clip(row, 0, ROWS - 1), 1), :] * jnp.where(owned, 1.0, 0.0)
                    value = jnp.where(sub == 4 * l + j, line, value)
            for k in range(3):
                stage[k, plane] = value[:, LANES * k : LANES * (k + 1)]

        @pl.loop(0, FIELDS)
        def _(f):
            window_rows(f, lambda l: state.at[f, l])

        @pl.loop(0, 2)
        def _(d):
            window_rows(FIELDS + d, lambda l: courant.at[d, l])

        place = iota((8, LANES), 1)

        @pl.loop(0, 3)
        def _(k):
            def pack_sides(plane, packed):
                low, high = packed
                value = stage[k, plane]
                here = (place >= 2 * plane) & (place < 2 * plane + 2)
                low = jnp.where(here, pltpu.roll(value, 2 * plane, 1), low)
                high = jnp.where(here, pltpu.roll(value, 2 * plane + 2, 1), high)
                return low, high

            empty = jnp.zeros((8, LANES), jnp.float32)
            low, high = lax.fori_loop(0, PLANES, pack_sides, (empty, empty))
            stage_side[k, 0] = high
            stage_side[k, 1] = low

    edge_targets = sum(
        jnp.where((tile - q + 1 - d >= 0) & (tile - q + 1 - d < groups), RATIO, 0) for d in range(4)
    )
    relay_targets = (
        sum(jnp.where(relay_tile(group + late) != tile, 1, 0) for late in range(2))
        + jnp.where(is_relay, 1, 0)
    )
    waited = len(NEAR) + pick(is_parent, edge_targets + jnp.where(in_window, 4, 0), relay_targets)
    pl.semaphore_wait(barrier, waited)

    def remote(source, target, send, recv, device):
        return pltpu.make_async_remote_copy(
            src_ref=source, dst_ref=target, send_sem=send, recv_sem=recv,
            device_id=device, device_id_type=MESH,
        )

    window_to = pick(at_top | low_window, 0, tiles - 1)
    window_slot = pick(low_window, tile - q + 1, tile - q - groups + 1)

    def window_copy(k):
        return remote(
            stage.at[k], window_in.at[window_slot], window_send.at[k], window_recv.at[window_slot],
            (window_to, 2 + RATIO * section + k),
        )

    def window_side_copy(k, side):
        return remote(
            stage_side.at[k, side], window_side.at[window_slot, side],
            window_send.at[3 + 2 * k + side], window_recv.at[3 + 2 * window_slot + side],
            (window_to, 2 + RATIO * section + k + 1 - 2 * side),
        )

    def for_windows(act):
        @pl.when(in_window)
        def _():
            @pl.loop(0, 3)
            def _(k):
                act(window_copy(k))
                for side in range(2):
                    aim = RATIO * section + k + 1 - 2 * side

                    @pl.when((aim >= 0) & (aim <= 5))
                    def _():
                        act(window_side_copy(k, side))

    for_windows(lambda copy: copy.start())

    def for_edges(act):
        @pl.when(is_parent)
        def _():
            @pl.loop(0, 4)
            def _(d):
                aim = tile - q + 1 - d

                @pl.when((aim >= 0) & (aim < groups))
                def _():
                    @pl.loop(0, RATIO)
                    def _(b):
                        act(
                            remote(
                                strips.at[section], edge_in.at[d], edge_send.at[d, b], edge_recv.at[d],
                                (aim * RATIO + b, pick(section == 0, 2, sections - 1)),
                            )
                        )

    for_edges(lambda copy: copy.start())

    def near_copy(i):
        source, target = (
            (slabs.at[0], near_slabs.at[0]),
            (slabs.at[1], near_slabs.at[1]),
            (strips.at[0], near_strips.at[0, 0:24]),
            (strips.at[0, 0:8], near_strips.at[0, 24:32]),
            (strips.at[0, 16:24], near_strips.at[0, 32:40]),
            (strips.at[1], near_strips.at[1, 0:24]),
            (strips.at[1, 0:8], near_strips.at[1, 24:32]),
            (strips.at[1, 16:24], near_strips.at[1, 32:40]),
        )[i]
        return remote(source, target, near_send.at[i], near_recv.at[i], near_peer(NEAR[i]))

    order = (2, 3, 4, 5, 6, 7, 0, 1)
    for i in order:
        near_copy(i).start()

    row = iota((TALL, WIDE), 0)
    col = iota((TALL, WIDE), 1)
    row = tile * ROWS + jnp.where(row < 28, row, row - TALL)
    col = pick(is_parent, section, nest) * COLS + jnp.where(col < 448, col, col - WIDE)
    last_row = tiles * ROWS - 1
    last_col = pick(is_parent, 2, 6) * COLS - 1
    depth = jnp.minimum(jnp.minimum(row, last_row - row), jnp.minimum(col, last_col - col))
    strength = pick(is_parent, 0.0, 1.0 / ZONE)
    mixed[0] = jnp.clip(ZONE - depth, 0, ZONE).astype(jnp.float32) * strength

    for i in order:
        near_copy(i).wait_recv()

    half = iota((8, LANES), 0) < 4
    beside = []
    for side in range(2):
        corner = jnp.where(half, near_strips[side, 24:32, :], near_strips[side, 32:40, :])
        beside.append(jnp.concatenate([near_strips[side, 0:24, :], corner], axis=0))
    from_right = iota((TALL, LANES), 1) < 64

    @pl.loop(0, PAIRS + 4)
    def _(i):
        g = i + jnp.where(i >= PAIRS + 2, PAIRS - 2, 0)
        right_part = pltpu.roll(beside[0], lax.rem(LANES - 3 * g, LANES), 1)
        left_part = pltpu.roll(beside[1], LANES - 3 * g - 3, 1)
        side_columns[i] = jnp.where(from_right, right_part, left_part)

    def whole(own, plane, l, sides):
        below, above = near_slabs[0, plane], near_slabs[1, plane]
        below = jnp.where(l == 0, below, pltpu.roll(below, 4, 0))
        above = jnp.where(l == 0, pltpu.roll(above, 4, 0), above)
        tall = jnp.concatenate([own, jnp.where(upper, below, above)], axis=0)
        return jnp.concatenate([tall, sides], axis=1)

    @pl.loop(0, LEVELS)
    def _(l):
        keep = 1.0 - mixed[0]
        speed_y, speed_x = (
            whole(courant[d, l], FIELDS + d, l, side_columns[PAIRS + 2 * d + l]) for d in range(2)
        )
        south = jnp.where(row == 0, 0.0, jnp.maximum(speed_y, 0.0) + DIFFUSION) * keep
        north = jnp.where(row == last_row, 0.0, DIFFUSION - jnp.minimum(speed_y, 0.0)) * keep
        west = jnp.where(col == 0, 0.0, jnp.maximum(speed_x, 0.0) + DIFFUSION) * keep
        east = jnp.where(col == last_col, 0.0, DIFFUSION - jnp.minimum(speed_x, 0.0)) * keep
        coef[l, 0] = (1.0 - MIXING) * keep - south - north - west - east
        coef[l, 1] = south
        coef[l, 2] = north
        coef[l, 3] = west
        coef[l, 4] = east
        mixed[1] = MIXING * keep

    @pl.when(rim_column)
    def _():
        for d in range(4):
            pltpu.make_async_copy(strips.at[0], edge_in.at[d], edge_recv.at[d]).wait()
        shape = (4 * ROWS, LANES)
        value = edge_in[...].reshape(shape)
        speed_y = pltpu.roll(value, LANES - 3 * PAIRS, 1)
        speed_x = pltpu.roll(value, LANES - 6 * PAIRS, 1)
        place = iota(shape, 1)
        trio = (place * 171) >> 9
        within = place - 3 * trio
        partner = jnp.where((trio & 1) == 0, pltpu.roll(value, LANES - 3, 1), pltpu.roll(value, 3, 1))
        change = (
            (jnp.maximum(speed_y, 0.0) + DIFFUSION) * (pltpu.roll(value, 1, 0) - value)
            + (DIFFUSION - jnp.minimum(speed_y, 0.0)) * (pltpu.roll(value, 4 * ROWS - 1, 0) - value)
            + jnp.where(within == 0, 0.0, jnp.maximum(speed_x, 0.0) + DIFFUSION) * (pltpu.roll(value, 1, 1) - value)
            + jnp.where(within == 2, 0.0, DIFFUSION - jnp.minimum(speed_x, 0.0))
            * (pltpu.roll(value, LANES - 1, 1) - value)
            + MIXING * (partner - value)
        ) * (1.0 / RATIO)
        wide = (TALL, 12 * ROWS)
        tall_row = iota(wide, 0)
        tall_row = jnp.where(tall_row < 28, tall_row, tall_row - TALL) + RATIO
        wanted = ((tall_row * 171) >> 9) - 1 + (ROWS + rest + COARSE * inner)
        source = iota(wide, 1)
        select = (source == wanted) | (source == wanted + 4 * ROWS) | (source == wanted + 8 * ROWS)
        both = jnp.concatenate([value, change], axis=1)
        rows = jnp.dot(
            jnp.where(select, 1.0, 0.0).astype(jnp.bfloat16),
            jnp.concatenate(thirds(both), axis=0),
            preferred_element_type=jnp.float32,
        )
        spread[0] = rows[:, :LANES]
        spread[1] = rows[:, LANES:]
        column = iota((TALL, LANES), 1)
        block = pl.ds(pl.multiple_of(pick(section == 2, 0, COLS - LANES), LANES), LANES)
        share = mixed[0, :, block]

        @pl.loop(0, PAIRS)
        def _(pair):
            for which, target in ((0, force), (1, slope)):
                turned = pltpu.roll(spread[which], lax.rem(LANES - 3 * pair, LANES), 1)
                lead, middle, trail = (
                    jnp.broadcast_to(turned[:, c : c + 1], (TALL, LANES)) for c in range(3)
                )
                filled = jnp.where(column < 3, lead, jnp.where(column < 125, middle, trail))
                target[pair, :, block] = share * filled

    @pl.when(rim_row)
    def _():
        @pl.loop(0, pick(at_top, 3, 2))
        def _(u):
            pltpu.make_async_copy(stage.at[0], window_in.at[u], window_recv.at[u]).wait()
            for side in range(2):
                @pl.when((nest - 1 + 2 * side >= 0) & (nest - 1 + 2 * side <= 5))
                def _():
                    pltpu.make_async_copy(
                        stage_side.at[0, side], window_side.at[u, side], window_recv.at[3 + 2 * u + side]
                    ).wait()

        sides = [window_side[0, side] + window_side[1, side] + window_side[2, side] for side in range(2)]

        def window(plane):
            centre = window_in[0, plane] + window_in[1, plane] + window_in[2, plane]
            before = pltpu.roll(sides[0], LANES - 2 * plane - 2, 1)
            after = pltpu.roll(sides[1], LANES - 2 * plane, 1) if plane else sides[1]
            return jnp.concatenate([before, centre, after], axis=1)

        speed_y, speed_x = window(FIELDS), window(FIELDS + 1)
        parent_col = iota((8, COLS), 1) + LANES * (nest - 1)
        south = jnp.maximum(speed_y, 0.0) + DIFFUSION
        north = DIFFUSION - jnp.minimum(speed_y, 0.0)
        west = jnp.where(parent_col == 0, 0.0, jnp.maximum(speed_x, 0.0) + DIFFUSION)
        east = jnp.where(parent_col == 2 * COLS - 1, 0.0, DIFFUSION - jnp.minimum(speed_x, 0.0))
        values, changes = [], []
        for f in range(FIELDS):
            value = window(f)
            change = (
                south * (pltpu.roll(value, 1, 0) - value)
                + north * (pltpu.roll(value, 7, 0) - value)
                + west * (pltpu.roll(value, 1, 1) - value)
                + east * (pltpu.roll(value, COLS - 1, 1) - value)
                + MIXING * (pltpu.roll(value, 4, 0) - value)
            ) * (1.0 / RATIO)
            values.append(value)
            changes.append(change)
        stacked = jnp.concatenate(values + changes, axis=0)
        sub = iota((8, LANES), 0)
        first = sub < pick(at_top, 3, 5)
        in_zone = (sub >= pick(at_top, 0, 3)) & (sub < pick(at_top, 5, 8))
        block = pl.ds(pl.multiple_of(pick(at_top, 0, 16), 8), 8)

        @pl.loop(0, 4)
        def _(k):
            column = iota((COLS, LANES), 1) + LANES * k
            column = jnp.where(column < 448, column, column - WIDE)
            ahead = column - RATIO * (iota((COLS, LANES), 0) - LANES)
            widen = jnp.where((ahead >= 0) & (ahead < RATIO), 1.0, 0.0).astype(jnp.bfloat16)
            rows = dot_ones(stacked, widen)
            lanes = pl.ds(pl.multiple_of(LANES * k, LANES), LANES)
            share = mixed[0, block, lanes]
            for which, target in ((0, force), (1, slope)):
                for pair in range(PAIRS):
                    f, l = pair // LEVELS, pair % LEVELS
                    at = 8 * (FIELDS * which + f) + 4 * l + 1
                    filled = jnp.where(first, rows[at : at + 1, :], rows[at + 1 : at + 2, :])
                    target[pair, block, lanes] = jnp.where(in_zone, share * filled, target[pair, block, lanes])

    ahead = iota((COLS, LANES), 0) - RATIO * iota((COLS, LANES), 1)
    gather = jnp.where((ahead >= 0) & (ahead < RATIO), 1.0, 0.0).astype(jnp.bfloat16)

    def for_relays(f, act, act_local):
        @pl.loop(0, 2)
        def _(late):
            target = relay_tile(group + late)

            @pl.when(target != tile)
            def _():
                act(
                    remote(
                        means.at[f], relay_in.at[f, late, inner], relay_send.at[f, late],
                        relay_recv.at[f, late, inner], (target, section),
                    )
                )

            if act_local is not None:
                @pl.when(target == tile)
                def _():
                    act_local(
                        pltpu.make_async_copy(
                            means.at[f], relay_in.at[f, late, inner], relay_recv.at[f, late, inner]
                        )
                    )

    steps = pick(is_parent, 1, RATIO)

    @pl.loop(0, FIELDS)
    def _(f):
        for l in range(LEVELS):
            work[l] = whole(state[f, l], f, l, side_columns[LEVELS * f + l])

        @pl.loop(0, steps)
        def _(k):
            fraction = (k + 1).astype(jnp.float32)
            pair = [work[l] for l in range(LEVELS)]
            mix = mixed[1]
            for l in range(LEVELS):
                value = pair[l]
                work[l] = (
                    coef[l, 0] * value
                    + coef[l, 1] * pltpu.roll(value, 1, 0)
                    + coef[l, 2] * pltpu.roll(value, TALL - 1, 0)
                    + coef[l, 3] * pltpu.roll(value, 1, 1)
                    + coef[l, 4] * pltpu.roll(value, WIDE - 1, 1)
                    + mix * pair[1 - l]
                    + (force[LEVELS * f + l] + fraction * slope[LEVELS * f + l])
                )

        for l in range(LEVELS):
            out[f, l] = work[l, :ROWS, :COLS]

        @pl.when(is_nest)
        def _():
            for l in range(LEVELS):
                for c in range(RATIO):
                    fine[c, l] = work[l, :ROWS, LANES * c : LANES * (c + 1)]
            sums = [
                sum(fine[c, :, pl.ds(k, COARSE, stride=RATIO), :] for k in range(RATIO))
                .reshape(LEVELS * COARSE, LANES)
                for c in range(RATIO)
            ]
            block = dot_ones(jnp.concatenate(sums, axis=1), gather) * (1.0 / (RATIO * RATIO))
            means[f] = block.reshape(LEVELS, COARSE, LANES)
            for_relays(f, lambda copy: copy.start(), lambda copy: copy.start())

    third = lax.rem(lax.max(nest, 0), RATIO)
    owner = lax.max(nest, 0) // RATIO

    def mean_copy(f):
        return remote(
            relay_out.at[f], mean_in.at[f, third], mean_send.at[f], mean_recv.at[f, third],
            (q + task, owner),
        )

    @pl.when(is_relay)
    def _():
        @pl.loop(0, FIELDS)
        def _(f):
            @pl.loop(0, 2)
            def _(late):
                @pl.when(relay_source(late))
                def _():
                    @pl.loop(0, RATIO)
                    def _(b):
                        pltpu.make_async_copy(
                            means.at[f], relay_in.at[f, late, b], relay_recv.at[f, late, b]
                        ).wait()
            for l in range(LEVELS):
                lined = jnp.concatenate(
                    [relay_in[f, late, b, l] for late in (1, 0) for b in range(RATIO)], axis=0
                )
                relay_out[f, l] = pltpu.roll(lined, rest + ROWS, 0)[:ROWS, :]
            mean_copy(f).start()

    @pl.when(under)
    def _():
        coarse_row = ROWS * (tile - q) - rest + iota((ROWS, COLS), 0)
        covered = (coarse_row >= 0) & (coarse_row < ROWS * groups)

        @pl.loop(0, FIELDS)
        def _(f):
            for c in range(RATIO):
                pltpu.make_async_copy(relay_out.at[f], mean_in.at[f, c], mean_recv.at[f, c]).wait()
            for l in range(LEVELS):
                fed = jnp.concatenate([mean_in[f, c, l] for c in range(RATIO)], axis=1)
                out[f, l] = jnp.where(covered, fed, out[f, l])

    for i in order:
        near_copy(i).wait_send()
    for_windows(lambda copy: copy.wait_send())
    for_edges(lambda copy: copy.wait_send())

    @pl.when(is_nest)
    def _():
        @pl.loop(0, FIELDS)
        def _(f):
            for_relays(f, lambda copy: copy.wait_send(), None)

    @pl.when(is_relay)
    def _():
        @pl.loop(0, FIELDS)
        def _(f):
            mean_copy(f).wait_send()


def solution(mesh):
    tiles = mesh.shape["tile"]
    sections = mesh.shape["section"]
    choices = max(tiles // 6 - 1, 4) - 1
    vmem = pl.BlockSpec(memory_space=pltpu.VMEM)
    anywhere = pl.BlockSpec(memory_space=pl.ANY)

    def call(q, state, courant, nest_offset):
        def space(*shape):
            return pltpu.VMEM(shape, jnp.float32)

        def copies(*shape):
            return pltpu.SemaphoreType.DMA(shape)

        return pl.pallas_call(
            functools.partial(kernel, q, tiles, sections),
            out_shape=jax.ShapeDtypeStruct(state.shape, state.dtype),
            in_specs=[pl.BlockSpec(memory_space=pltpu.SMEM), anywhere, anywhere],
            out_specs=vmem,
            scratch_shapes=[
                space(FIELDS, LEVELS, ROWS, COLS),
                space(2, LEVELS, ROWS, COLS),
                space(2, ROWS, LANES),
                space(2, ROWS + 16, LANES),
                space(2, PLANES, 8, COLS),
                space(2, PLANES, 8, COLS),
                space(PAIRS + 4, TALL, LANES),
                space(4, ROWS, LANES),
                space(2, TALL, LANES),
                space(3, PLANES, 8, LANES),
                space(3, 2, 8, LANES),
                space(3, PLANES, 8, LANES),
                space(3, 2, 8, LANES),
                space(LEVELS, 5, TALL, WIDE),
                space(2, TALL, WIDE),
                space(PAIRS, TALL, WIDE),
                space(PAIRS, TALL, WIDE),
                space(LEVELS, TALL, WIDE),
                space(RATIO, LEVELS, ROWS, LANES),
                space(FIELDS, LEVELS, COARSE, LANES),
                space(FIELDS, 2, RATIO, LEVELS, COARSE, LANES),
                space(FIELDS, LEVELS, ROWS, LANES),
                space(FIELDS, RATIO, LEVELS, ROWS, LANES),
                copies(2), copies(8), copies(8), copies(4, RATIO), copies(4),
                copies(9), copies(9), copies(FIELDS, 2), copies(FIELDS, 2, RATIO),
                copies(FIELDS), copies(FIELDS, RATIO),
            ],
            compiler_params=pltpu.CompilerParams(collective_id=q, has_side_effects=True),
            name=f"nested_step_{q}",
        )(nest_offset, state, courant)

    def on_device(state, courant, nest_offset):
        branches = [functools.partial(call, q) for q in range(1, choices + 1)]
        choice = jnp.clip(nest_offset[0] // ROWS - 1, 0, choices - 1)
        return lax.switch(choice, branches, state, courant, nest_offset)

    return jax.shard_map(
        on_device,
        mesh=mesh,
        in_specs=(P(None, None, "tile", "section"), P(None, None, "tile", "section"), P()),
        out_specs=P(None, None, "tile", "section"),
        check_vma=False,
    )
```

profile of v0, /device:TPU:88, one launch (start us, length us, event | category | flops | bytes accessed | tf_op | source)
XLA Modules:
  0.0 47.1 jit_solution(8154423678144198539)
XLA Ops:
  0.7 45.7 %conditional.1 = (f32[5,2,24,384]{3,2,1,0:T(8,128)S(1)}) conditional(s32[]{:T(128)} %clamp.3, (s32[1]{0:T(128)}, f32[5,2,24,384]{3,2,1,0:T(8,128)}, f32[2,2,24,384]{3,2,1,0:T(8,128)}) %tuple.47, (s32[1]{0:T(128)}, f32[5,2,24,384]{3,2,1,0:T(8,128)}, f32[2,2,24,384]{3,2,1,0:T(8,128)}) %tuple.47, (s32[1]{0:T(128)}, ...), branch_computations={%region_0.1_spmd, %region_1.2_spmd, %region_2.3_spmd, %region_3.4_... | conditional | bytes 8 | solution.py:663
  0.7 45.3 %nested_step_4.1 = f32[5,2,24,384]{3,2,1,0:T(8,128)S(1)} custom-call(s32[1]{0:T(128)} %get-tuple-element.107.offset_ref, f32[5,2,24,384]{3,2,1,0:T(8,128)} %get-tuple-element.112.state_in, f32[2,2,24,384]{3,2,1,0:T(8,128)} %get-tuple-element.114.courant_in), custom_call_target="tpu_custom_call" | custom-call | tf_op jit(solution)/shard_map/cond/branch_3_fun/nested_step_4/pallas_call | solution.py:623
  46.3 0.7 %copy.34 = f32[5,2,24,384]{3,2,1,0:T(8,128)} copy(f32[5,2,24,384]{3,2,1,0:T(8,128)S(1)} %get-tuple-element.146) | data formatting | bytes 737280
where the time goes:
time: 47.2 us; the launch traced here: 47.1 us
  Pallas kernels  45.3 us (96%)
  local copies, waits for them, and re-layouts  0.74 us (2%)
  between operations  0.69 us (1%)
    pallas_call x1, Pallas kernels, call(): pl.pallas_call(functools.partial(kernel, q, tiles, sections), out_shape=j...  45.3 us

commit v1 on v0

--- a/solution.py
+++ b/solution.py
@@ -52,9 +52,11 @@
     q, tiles, sections,
     offset_ref, state_in, courant_in, out,
     state, courant, strips, near_strips, slabs, near_slabs, side_columns,
-    edge_in, spread, stage, stage_side, window_in, window_side, coef, mixed, force, slope, work,
+    edge_in, spread, spread_in, stage, window_in, rows_out, rows_in,
+    coef, mixed, force, slope, work,
     fine, means, relay_in, relay_out, mean_in,
     load_sem, near_send, near_recv, edge_send, edge_recv, window_send, window_recv,
+    spread_send, spread_recv, rows_send, rows_recv, edge_ready, rows_ready,
     relay_send, relay_recv, mean_send, mean_recv,
 ):
     tile = lax.axis_index("tile")
@@ -68,11 +70,21 @@
     rest = offset_ref[0] - q * ROWS
     rim_column = (section == 2) | (section == sections - 1)
     at_top = tile == 0
-    rim_row = is_nest & (at_top | (tile == tiles - 1))
+    at_end = at_top | (tile == tiles - 1)
+    rim_row = is_nest & at_end
+    row_relay = is_parent & at_end
+    has_left = (section != 0) & (section != 2)
+    has_right = (section != 1) & (section != sections - 1)
     low_window = is_parent & (tile >= q - 1) & (tile <= q + 1)
     high_window = is_parent & (tile >= q + groups - 1) & (tile <= q + groups)
     in_window = low_window | high_window
+    window_to = pick(low_window, 0, tiles - 1)
+    window_slot = pick(low_window, tile - q + 1, tile - q - groups + 1)
+    window_first = pick(at_top, q - 1, q + groups - 1)
+    window_count = pick(at_top, 3, 2)
     under = is_parent & (tile >= q) & (tile <= q + groups)
+    third = lax.rem(lax.max(nest, 0), RATIO)
+    owner = lax.max(nest, 0) // RATIO
 
     def relay_tile(a):
         return lax.min(a, groups - 1) * RATIO // groups * groups + lax.rem(q + a, groups)
@@ -83,10 +95,7 @@
     is_relay = is_nest & (relay_tile(task) == tile)
 
     def near_peer(step):
-        return (
-            lax.rem(tile + step[0] + tiles, tiles),
-            lax.rem(section + step[1] + sections, sections),
-        )
+        return lax.rem(tile + step[0] + tiles, tiles), section + step[1]
 
     loads = [
         pltpu.make_async_copy(state_in, state, load_sem.at[0]),
@@ -95,12 +104,15 @@
     for load in loads:
         load.start()
 
-    @pl.when(rim_row)
+    @pl.when(row_relay)
     def _():
         @pl.loop(0, 3)
         def _(u):
-            window_in[u] = jnp.zeros((PLANES, 8, LANES), jnp.float32)
-            window_side[u] = jnp.zeros((2, 8, LANES), jnp.float32)
+            @pl.loop(0, 5)
+            def _(slot):
+                window_in[u, slot] = jnp.zeros((PLANES, 8, LANES), jnp.float32)
+
+    near_strips[...] = jnp.zeros_like(near_strips)
 
     barrier = pltpu.get_barrier_semaphore()
 
@@ -109,28 +121,46 @@
             barrier, inc=1, device_id=(tile_to, section_to), device_id_type=MESH
         )
 
-    @pl.when(rim_column)
-    def _():
+    rim_section = pick(section == 0, 2, sections - 1)
+
+    @pl.when(is_parent)
+    def _():
+        greet(tile, rim_section)
+
         @pl.loop(0, 4)
         def _(d):
-            greet(q + group + d - 1, pick(section == 2, 0, 1))
-
-    @pl.when(rim_row)
-    def _():
-        @pl.loop(0, pick(at_top, 3, 2))
+            sender = q + group + d - 1
+
+            @pl.when(sender != tile)
+            def _():
+                greet(sender, section)
+
+    @pl.when(row_relay)
+    def _():
+        @pl.loop(0, RATIO)
+        def _(k):
+            greet(tile, 2 + RATIO * section + k)
+
+        @pl.loop(0, window_count)
         def _(u):
-            sender = pick(at_top, q - 1, q + groups - 1) + u
-
-            @pl.when(nest <= 3)
+            greet(window_first + u, 1 - section)
+
+            @pl.when(window_first + u != tile)
             def _():
-                greet(sender, 0)
-
-            @pl.when(nest >= 2)
-            def _():
-                greet(sender, 1)
-
-    for step in NEAR:
+                greet(window_first + u, section)
+
+    for step in NEAR[:2]:
         greet(*near_peer(step))
+
+    @pl.when(has_left)
+    def _():
+        for step in NEAR[2:5]:
+            greet(*near_peer(step))
+
+    @pl.when(has_right)
+    def _():
+        for step in NEAR[5:]:
+            greet(*near_peer(step))
 
     def relay_source(late):
         return (task - late >= 0) & (task - late < groups)
@@ -219,32 +249,31 @@
         def _(d):
             window_rows(FIELDS + d, lambda l: courant.at[d, l])
 
-        place = iota((8, LANES), 1)
-
-        @pl.loop(0, 3)
-        def _(k):
-            def pack_sides(plane, packed):
-                low, high = packed
-                value = stage[k, plane]
-                here = (place >= 2 * plane) & (place < 2 * plane + 2)
-                low = jnp.where(here, pltpu.roll(value, 2 * plane, 1), low)
-                high = jnp.where(here, pltpu.roll(value, 2 * plane + 2, 1), high)
-                return low, high
-
-            empty = jnp.zeros((8, LANES), jnp.float32)
-            low, high = lax.fori_loop(0, PLANES, pack_sides, (empty, empty))
-            stage_side[k, 0] = high
-            stage_side[k, 1] = low
-
     edge_targets = sum(
-        jnp.where((tile - q + 1 - d >= 0) & (tile - q + 1 - d < groups), RATIO, 0) for d in range(4)
+        jnp.where((tile - q + 1 - d >= 0) & (tile - q + 1 - d < groups), RATIO, 0)
+        - jnp.where(tile - q + 1 - d == group, 1, 0)
+        for d in range(4)
     )
+    window_targets = jnp.where(in_window, 1, 0) + jnp.where(in_window & (window_to != tile), 1, 0)
     relay_targets = (
         sum(jnp.where(relay_tile(group + late) != tile, 1, 0) for late in range(2))
         + jnp.where(is_relay, 1, 0)
+        + jnp.where(rim_column, 1, 0)
+        + jnp.where(rim_row, 1, 0)
     )
-    waited = len(NEAR) + pick(is_parent, edge_targets + jnp.where(in_window, 4, 0), relay_targets)
+    near_targets = 2 + jnp.where(has_left, 3, 0) + jnp.where(has_right, 3, 0)
+    waited = near_targets + pick(is_parent, edge_targets + window_targets, relay_targets)
     pl.semaphore_wait(barrier, waited)
+
+    @pl.when(rim_column)
+    def _():
+        pl.semaphore_signal(
+            edge_ready, inc=1, device_id=(tile, pick(section == 2, 0, 1)), device_id_type=MESH
+        )
+
+    @pl.when(rim_row)
+    def _():
+        pl.semaphore_signal(rows_ready.at[third], inc=1, device_id=(tile, owner), device_id_type=MESH)
 
     def remote(source, target, send, recv, device):
         return pltpu.make_async_remote_copy(
@@ -252,38 +281,38 @@
             device_id=device, device_id_type=MESH,
         )
 
-    window_to = pick(at_top | low_window, 0, tiles - 1)
-    window_slot = pick(low_window, tile - q + 1, tile - q - groups + 1)
-
-    def window_copy(k):
-        return remote(
-            stage.at[k], window_in.at[window_slot], window_send.at[k], window_recv.at[window_slot],
-            (window_to, 2 + RATIO * section + k),
-        )
-
-    def window_side_copy(k, side):
-        return remote(
-            stage_side.at[k, side], window_side.at[window_slot, side],
-            window_send.at[3 + 2 * k + side], window_recv.at[3 + 2 * window_slot + side],
-            (window_to, 2 + RATIO * section + k + 1 - 2 * side),
-        )
-
-    def for_windows(act):
+    def start(copy):
+        copy.start()
+
+    def wait_send(copy):
+        copy.wait_send()
+
+    def for_windows(act, act_local):
         @pl.when(in_window)
         def _():
-            @pl.loop(0, 3)
-            def _(k):
-                act(window_copy(k))
-                for side in range(2):
-                    aim = RATIO * section + k + 1 - 2 * side
-
-                    @pl.when((aim >= 0) & (aim <= 5))
-                    def _():
-                        act(window_side_copy(k, side))
-
-    for_windows(lambda copy: copy.start())
-
-    def for_edges(act):
+            target = window_in.at[window_slot, 1:4]
+            arrived = window_recv.at[window_slot, 0]
+
+            @pl.when(window_to != tile)
+            def _():
+                act(remote(stage, target, window_send.at[0], arrived, (window_to, section)))
+
+            if act_local is not None:
+                @pl.when(window_to == tile)
+                def _():
+                    act_local(pltpu.make_async_copy(stage, target, arrived))
+
+            act(
+                remote(
+                    stage.at[pick(section == 0, 2, 0)],
+                    window_in.at[window_slot, pick(section == 0, 0, 4)],
+                    window_send.at[1], window_recv.at[window_slot, 1], (window_to, 1 - section),
+                )
+            )
+
+    for_windows(start, start)
+
+    def for_edges(act, act_local):
         @pl.when(is_parent)
         def _():
             @pl.loop(0, 4)
@@ -294,14 +323,25 @@
                 def _():
                     @pl.loop(0, RATIO)
                     def _(b):
-                        act(
-                            remote(
-                                strips.at[section], edge_in.at[d], edge_send.at[d, b], edge_recv.at[d],
-                                (aim * RATIO + b, pick(section == 0, 2, sections - 1)),
+                        target = aim * RATIO + b
+
+                        @pl.when(target != tile)
+                        def _():
+                            act(
+                                remote(
+                                    strips.at[section], edge_in.at[d], edge_send.at[d, b],
+                                    edge_recv.at[d], (target, section),
+                                )
                             )
-                        )
-
-    for_edges(lambda copy: copy.start())
+
+                        if act_local is not None:
+                            @pl.when(target == tile)
+                            def _():
+                                act_local(
+                                    pltpu.make_async_copy(strips.at[section], edge_in.at[d], edge_recv.at[d])
+                                )
+
+    for_edges(start, start)
 
     def near_copy(i):
         source, target = (
@@ -316,62 +356,31 @@
         )[i]
         return remote(source, target, near_send.at[i], near_recv.at[i], near_peer(NEAR[i]))
 
-    order = (2, 3, 4, 5, 6, 7, 0, 1)
-    for i in order:
-        near_copy(i).start()
-
-    row = iota((TALL, WIDE), 0)
-    col = iota((TALL, WIDE), 1)
-    row = tile * ROWS + jnp.where(row < 28, row, row - TALL)
-    col = pick(is_parent, section, nest) * COLS + jnp.where(col < 448, col, col - WIDE)
-    last_row = tiles * ROWS - 1
-    last_col = pick(is_parent, 2, 6) * COLS - 1
-    depth = jnp.minimum(jnp.minimum(row, last_row - row), jnp.minimum(col, last_col - col))
-    strength = pick(is_parent, 0.0, 1.0 / ZONE)
-    mixed[0] = jnp.clip(ZONE - depth, 0, ZONE).astype(jnp.float32) * strength
-
-    for i in order:
-        near_copy(i).wait_recv()
-
-    half = iota((8, LANES), 0) < 4
-    beside = []
-    for side in range(2):
-        corner = jnp.where(half, near_strips[side, 24:32, :], near_strips[side, 32:40, :])
-        beside.append(jnp.concatenate([near_strips[side, 0:24, :], corner], axis=0))
-    from_right = iota((TALL, LANES), 1) < 64
-
-    @pl.loop(0, PAIRS + 4)
-    def _(i):
-        g = i + jnp.where(i >= PAIRS + 2, PAIRS - 2, 0)
-        right_part = pltpu.roll(beside[0], lax.rem(LANES - 3 * g, LANES), 1)
-        left_part = pltpu.roll(beside[1], LANES - 3 * g - 3, 1)
-        side_columns[i] = jnp.where(from_right, right_part, left_part)
-
-    def whole(own, plane, l, sides):
-        below, above = near_slabs[0, plane], near_slabs[1, plane]
-        below = jnp.where(l == 0, below, pltpu.roll(below, 4, 0))
-        above = jnp.where(l == 0, pltpu.roll(above, 4, 0), above)
-        tall = jnp.concatenate([own, jnp.where(upper, below, above)], axis=0)
-        return jnp.concatenate([tall, sides], axis=1)
-
-    @pl.loop(0, LEVELS)
-    def _(l):
-        keep = 1.0 - mixed[0]
-        speed_y, speed_x = (
-            whole(courant[d, l], FIELDS + d, l, side_columns[PAIRS + 2 * d + l]) for d in range(2)
+    def for_near(act, left_exists, right_exists):
+        @pl.when(left_exists)
+        def _():
+            for i in (2, 3, 4):
+                act(near_copy(i))
+
+        @pl.when(right_exists)
+        def _():
+            for i in (5, 6, 7):
+                act(near_copy(i))
+
+        for i in (0, 1):
+            act(near_copy(i))
+
+    for_near(start, has_left, has_right)
+
+    def spread_copy():
+        return remote(spread, spread_in, spread_send, spread_recv, (tile, rim_section))
+
+    def rows_copy(k):
+        return remote(
+            rows_out.at[k], rows_in, rows_send.at[k], rows_recv, (tile, 2 + RATIO * section + k)
         )
-        south = jnp.where(row == 0, 0.0, jnp.maximum(speed_y, 0.0) + DIFFUSION) * keep
-        north = jnp.where(row == last_row, 0.0, DIFFUSION - jnp.minimum(speed_y, 0.0)) * keep
-        west = jnp.where(col == 0, 0.0, jnp.maximum(speed_x, 0.0) + DIFFUSION) * keep
-        east = jnp.where(col == last_col, 0.0, DIFFUSION - jnp.minimum(speed_x, 0.0)) * keep
-        coef[l, 0] = (1.0 - MIXING) * keep - south - north - west - east
-        coef[l, 1] = south
-        coef[l, 2] = north
-        coef[l, 3] = west
-        coef[l, 4] = east
-        mixed[1] = MIXING * keep
-
-    @pl.when(rim_column)
+
+    @pl.when(is_parent)
     def _():
         for d in range(4):
             pltpu.make_async_copy(strips.at[0], edge_in.at[d], edge_recv.at[d]).wait()
@@ -405,6 +414,112 @@
         )
         spread[0] = rows[:, :LANES]
         spread[1] = rows[:, LANES:]
+        pl.semaphore_wait(edge_ready, 1)
+        spread_copy().start()
+
+    @pl.when(row_relay)
+    def _():
+        @pl.loop(0, window_count)
+        def _(u):
+            beside_slot = pick(section == 0, 4, 0)
+            pltpu.make_async_copy(stage, window_in.at[u, 1:4], window_recv.at[u, 0]).wait()
+            pltpu.make_async_copy(stage.at[0], window_in.at[u, beside_slot], window_recv.at[u, 1]).wait()
+
+        def window(plane):
+            return jnp.concatenate([sum(window_in[u, k, plane] for u in range(3)) for k in range(5)], axis=1)
+
+        shape = (8, 5 * LANES)
+        speed_y, speed_x = window(FIELDS), window(FIELDS + 1)
+        parent_col = iota(shape, 1) + (COLS * section - LANES)
+        south = jnp.maximum(speed_y, 0.0) + DIFFUSION
+        north = DIFFUSION - jnp.minimum(speed_y, 0.0)
+        west = jnp.where(parent_col == 0, 0.0, jnp.maximum(speed_x, 0.0) + DIFFUSION)
+        east = jnp.where(parent_col == 2 * COLS - 1, 0.0, DIFFUSION - jnp.minimum(speed_x, 0.0))
+        within = iota(shape, 0) & 3
+        is_value = (within == 1) | (within == 2)
+
+        @pl.loop(0, FIELDS)
+        def _(f):
+            value = window(f)
+            change = (
+                south * (pltpu.roll(value, 1, 0) - value)
+                + north * (pltpu.roll(value, 7, 0) - value)
+                + west * (pltpu.roll(value, 1, 1) - value)
+                + east * (pltpu.roll(value, 5 * LANES - 1, 1) - value)
+                + MIXING * (pltpu.roll(value, 4, 0) - value)
+            ) * (1.0 / RATIO)
+            both = jnp.where(is_value, value, pltpu.roll(change, 2, 0))
+            for k in range(RATIO):
+                rows_out[k, f, :, 0:COLS] = both[:, LANES * k : LANES * k + COLS]
+
+        stacked = rows_out[:, :, :, 0:COLS].reshape(RATIO * FIELDS * 8, COLS)
+
+        @pl.loop(0, WIDE // LANES)
+        def _(k):
+            column = iota((COLS, LANES), 1) + LANES * k
+            column = jnp.where(column < 448, column, column - WIDE)
+            ahead = column - RATIO * (iota((COLS, LANES), 0) - LANES)
+            widen = jnp.where((ahead >= 0) & (ahead < RATIO), 1.0, 0.0).astype(jnp.bfloat16)
+            lanes = pl.ds(pl.multiple_of(LANES * k, LANES), LANES)
+            rows_out[:, :, :, lanes] = dot_ones(stacked, widen).reshape(RATIO, FIELDS, 8, LANES)
+
+        @pl.loop(0, RATIO)
+        def _(k):
+            pl.semaphore_wait(rows_ready.at[k], 1)
+            rows_copy(k).start()
+    row = iota((TALL, WIDE), 0)
+    col = iota((TALL, WIDE), 1)
+    row = tile * ROWS + jnp.where(row < 28, row, row - TALL)
+    col = pick(is_parent, section, nest) * COLS + jnp.where(col < 448, col, col - WIDE)
+    last_row = tiles * ROWS - 1
+    last_col = pick(is_parent, 2, 6) * COLS - 1
+    depth = jnp.minimum(jnp.minimum(row, last_row - row), jnp.minimum(col, last_col - col))
+    strength = pick(is_parent, 0.0, 1.0 / ZONE)
+    mixed[0] = jnp.clip(ZONE - depth, 0, ZONE).astype(jnp.float32) * strength
+
+    for_near(lambda copy: copy.wait_recv(), has_right, has_left)
+
+    half = iota((8, LANES), 0) < 4
+    beside = []
+    for side in range(2):
+        corner = jnp.where(half, near_strips[side, 24:32, :], near_strips[side, 32:40, :])
+        beside.append(jnp.concatenate([near_strips[side, 0:24, :], corner], axis=0))
+    from_right = iota((TALL, LANES), 1) < 64
+
+    @pl.loop(0, PAIRS + 4)
+    def _(i):
+        g = i + jnp.where(i >= PAIRS + 2, PAIRS - 2, 0)
+        right_part = pltpu.roll(beside[0], lax.rem(LANES - 3 * g, LANES), 1)
+        left_part = pltpu.roll(beside[1], LANES - 3 * g - 3, 1)
+        side_columns[i] = jnp.where(from_right, right_part, left_part)
+
+    def whole(own, plane, l, sides):
+        below, above = near_slabs[0, plane], near_slabs[1, plane]
+        below = jnp.where(l == 0, below, pltpu.roll(below, 4, 0))
+        above = jnp.where(l == 0, pltpu.roll(above, 4, 0), above)
+        tall = jnp.concatenate([own, jnp.where(upper, below, above)], axis=0)
+        return jnp.concatenate([tall, sides], axis=1)
+
+    @pl.loop(0, LEVELS)
+    def _(l):
+        keep = 1.0 - mixed[0]
+        speed_y, speed_x = (
+            whole(courant[d, l], FIELDS + d, l, side_columns[PAIRS + 2 * d + l]) for d in range(2)
+        )
+        south = jnp.where(row == 0, 0.0, jnp.maximum(speed_y, 0.0) + DIFFUSION) * keep
+        north = jnp.where(row == last_row, 0.0, DIFFUSION - jnp.minimum(speed_y, 0.0)) * keep
+        west = jnp.where(col == 0, 0.0, jnp.maximum(speed_x, 0.0) + DIFFUSION) * keep
+        east = jnp.where(col == last_col, 0.0, DIFFUSION - jnp.minimum(speed_x, 0.0)) * keep
+        coef[l, 0] = (1.0 - MIXING) * keep - south - north - west - east
+        coef[l, 1] = south
+        coef[l, 2] = north
+        coef[l, 3] = west
+        coef[l, 4] = east
+        mixed[1] = MIXING * keep
+
+    @pl.when(rim_column)
+    def _():
+        pltpu.make_async_copy(spread, spread_in, spread_recv).wait()
         column = iota((TALL, LANES), 1)
         block = pl.ds(pl.multiple_of(pick(section == 2, 0, COLS - LANES), LANES), LANES)
         share = mixed[0, :, block]
@@ -412,7 +527,7 @@
         @pl.loop(0, PAIRS)
         def _(pair):
             for which, target in ((0, force), (1, slope)):
-                turned = pltpu.roll(spread[which], lax.rem(LANES - 3 * pair, LANES), 1)
+                turned = pltpu.roll(spread_in[which], lax.rem(LANES - 3 * pair, LANES), 1)
                 lead, middle, trail = (
                     jnp.broadcast_to(turned[:, c : c + 1], (TALL, LANES)) for c in range(3)
                 )
@@ -421,63 +536,21 @@
 
     @pl.when(rim_row)
     def _():
-        @pl.loop(0, pick(at_top, 3, 2))
-        def _(u):
-            pltpu.make_async_copy(stage.at[0], window_in.at[u], window_recv.at[u]).wait()
-            for side in range(2):
-                @pl.when((nest - 1 + 2 * side >= 0) & (nest - 1 + 2 * side <= 5))
-                def _():
-                    pltpu.make_async_copy(
-                        stage_side.at[0, side], window_side.at[u, side], window_recv.at[3 + 2 * u + side]
-                    ).wait()
-
-        sides = [window_side[0, side] + window_side[1, side] + window_side[2, side] for side in range(2)]
-
-        def window(plane):
-            centre = window_in[0, plane] + window_in[1, plane] + window_in[2, plane]
-            before = pltpu.roll(sides[0], LANES - 2 * plane - 2, 1)
-            after = pltpu.roll(sides[1], LANES - 2 * plane, 1) if plane else sides[1]
-            return jnp.concatenate([before, centre, after], axis=1)
-
-        speed_y, speed_x = window(FIELDS), window(FIELDS + 1)
-        parent_col = iota((8, COLS), 1) + LANES * (nest - 1)
-        south = jnp.maximum(speed_y, 0.0) + DIFFUSION
-        north = DIFFUSION - jnp.minimum(speed_y, 0.0)
-        west = jnp.where(parent_col == 0, 0.0, jnp.maximum(speed_x, 0.0) + DIFFUSION)
-        east = jnp.where(parent_col == 2 * COLS - 1, 0.0, DIFFUSION - jnp.minimum(speed_x, 0.0))
-        values, changes = [], []
-        for f in range(FIELDS):
-            value = window(f)
-            change = (
-                south * (pltpu.roll(value, 1, 0) - value)
-                + north * (pltpu.roll(value, 7, 0) - value)
-                + west * (pltpu.roll(value, 1, 1) - value)
-                + east * (pltpu.roll(value, COLS - 1, 1) - value)
-                + MIXING * (pltpu.roll(value, 4, 0) - value)
-            ) * (1.0 / RATIO)
-            values.append(value)
-            changes.append(change)
-        stacked = jnp.concatenate(values + changes, axis=0)
-        sub = iota((8, LANES), 0)
+        pltpu.make_async_copy(rows_out.at[0], rows_in, rows_recv).wait()
+        sub = iota((8, WIDE), 0)
         first = sub < pick(at_top, 3, 5)
         in_zone = (sub >= pick(at_top, 0, 3)) & (sub < pick(at_top, 5, 8))
         block = pl.ds(pl.multiple_of(pick(at_top, 0, 16), 8), 8)
-
-        @pl.loop(0, 4)
-        def _(k):
-            column = iota((COLS, LANES), 1) + LANES * k
-            column = jnp.where(column < 448, column, column - WIDE)
-            ahead = column - RATIO * (iota((COLS, LANES), 0) - LANES)
-            widen = jnp.where((ahead >= 0) & (ahead < RATIO), 1.0, 0.0).astype(jnp.bfloat16)
-            rows = dot_ones(stacked, widen)
-            lanes = pl.ds(pl.multiple_of(LANES * k, LANES), LANES)
-            share = mixed[0, block, lanes]
-            for which, target in ((0, force), (1, slope)):
-                for pair in range(PAIRS):
-                    f, l = pair // LEVELS, pair % LEVELS
-                    at = 8 * (FIELDS * which + f) + 4 * l + 1
-                    filled = jnp.where(first, rows[at : at + 1, :], rows[at + 1 : at + 2, :])
-                    target[pair, block, lanes] = jnp.where(in_zone, share * filled, target[pair, block, lanes])
+        share = mixed[0, block, :]
+
+        @pl.loop(0, FIELDS)
+        def _(f):
+            rows = rows_in[f]
+            for l in range(LEVELS):
+                for target, one, two in ((force, 4 * l + 1, 4 * l + 2), (slope, 4 * l + 3, (4 * l + 4) % 8)):
+                    filled = jnp.where(first, rows[one : one + 1, :], rows[two : two + 1, :])
+                    old = target[LEVELS * f + l, block, :]
+                    target[LEVELS * f + l, block, :] = jnp.where(in_zone, share * filled, old)
 
     ahead = iota((COLS, LANES), 0) - RATIO * iota((COLS, LANES), 1)
     gather = jnp.where((ahead >= 0) & (ahead < RATIO), 1.0, 0.0).astype(jnp.bfloat16)
@@ -544,10 +617,7 @@
             ]
             block = dot_ones(jnp.concatenate(sums, axis=1), gather) * (1.0 / (RATIO * RATIO))
             means[f] = block.reshape(LEVELS, COARSE, LANES)
-            for_relays(f, lambda copy: copy.start(), lambda copy: copy.start())
-
-    third = lax.rem(lax.max(nest, 0), RATIO)
-    owner = lax.max(nest, 0) // RATIO
+            for_relays(f, start, start)
 
     def mean_copy(f):
         return remote(
@@ -588,16 +658,25 @@
                 fed = jnp.concatenate([mean_in[f, c, l] for c in range(RATIO)], axis=1)
                 out[f, l] = jnp.where(covered, fed, out[f, l])
 
-    for i in order:
-        near_copy(i).wait_send()
-    for_windows(lambda copy: copy.wait_send())
-    for_edges(lambda copy: copy.wait_send())
+    for_near(wait_send, has_left, has_right)
+    for_windows(wait_send, None)
+    for_edges(wait_send, None)
+
+    @pl.when(is_parent)
+    def _():
+        spread_copy().wait_send()
+
+    @pl.when(row_relay)
+    def _():
+        @pl.loop(0, RATIO)
+        def _(k):
+            rows_copy(k).wait_send()
 
     @pl.when(is_nest)
     def _():
         @pl.loop(0, FIELDS)
         def _(f):
-            for_relays(f, lambda copy: copy.wait_send(), None)
+            for_relays(f, wait_send, None)
 
     @pl.when(is_relay)
     def _():
@@ -635,10 +714,11 @@
                 space(PAIRS + 4, TALL, LANES),
                 space(4, ROWS, LANES),
                 space(2, TALL, LANES),
+                space(2, TALL, LANES),
                 space(3, PLANES, 8, LANES),
-                space(3, 2, 8, LANES),
-                space(3, PLANES, 8, LANES),
-                space(3, 2, 8, LANES),
+                space(3, 5, PLANES, 8, LANES),
+                space(RATIO, FIELDS, 8, WIDE),
+                space(FIELDS, 8, WIDE),
                 space(LEVELS, 5, TALL, WIDE),
                 space(2, TALL, WIDE),
                 space(PAIRS, TALL, WIDE),
@@ -649,9 +729,10 @@
                 space(FIELDS, 2, RATIO, LEVELS, COARSE, LANES),
                 space(FIELDS, LEVELS, ROWS, LANES),
                 space(FIELDS, RATIO, LEVELS, ROWS, LANES),
-                copies(2), copies(8), copies(8), copies(4, RATIO), copies(4),
-                copies(9), copies(9), copies(FIELDS, 2), copies(FIELDS, 2, RATIO),
-                copies(FIELDS), copies(FIELDS, RATIO),
+                copies(2), copies(8), copies(8), copies(4, RATIO), copies(4), copies(2), copies(3, 2),
+                pltpu.SemaphoreType.DMA, pltpu.SemaphoreType.DMA, copies(RATIO), pltpu.SemaphoreType.DMA,
+                pltpu.SemaphoreType.REGULAR, pltpu.SemaphoreType.REGULAR((RATIO,)),
+                copies(FIELDS, 2), copies(FIELDS, 2, RATIO), copies(FIELDS), copies(FIELDS, RATIO),
             ],
             compiler_params=pltpu.CompilerParams(collective_id=q, has_side_effects=True),
             name=f"nested_step_{q}",

time: 47.2 us -> 49.6 us (1.051)
  the two profiles are of different devices: /device:TPU:88 before, /device:TPU:34 now
where the time goes in v1:
time: 49.6 us; the launch traced here: 49.5 us
  Pallas kernels  47.8 us (96%)
  local copies, waits for them, and re-layouts  0.74 us (1%)
  between operations  0.69 us (1%)
    pallas_call x1, Pallas kernels, call(): pl.pallas_call(functools.partial(kernel, q, tiles, sections), out_shape=j...  47.8 us

profile of v1, /device:TPU:34, one launch (start us, length us, event | category | flops | bytes accessed | tf_op | source)
XLA Modules:
  0.0 49.5 jit_solution(13548333682720403495)
XLA Ops:
  0.7 48.1 %conditional.1 = (f32[5,2,24,384]{3,2,1,0:T(8,128)S(1)}) conditional(s32[]{:T(128)} %clamp.3, (s32[1]{0:T(128)}, f32[5,2,24,384]{3,2,1,0:T(8,128)}, f32[2,2,24,384]{3,2,1,0:T(8,128)}) %tuple.47, (s32[1]{0:T(128)}, f32[5,2,24,384]{3,2,1,0:T(8,128)}, f32[2,2,24,384]{3,2,1,0:T(8,128)}) %tuple.47, (s32[1]{0:T(128)}, ...), branch_computations={%region_0.1_spmd, %region_1.2_spmd, %region_2.3_spmd, %region_3.4_... | conditional | bytes 8 | solution.py:744
  0.9 47.8 %nested_step_12.1 = f32[5,2,24,384]{3,2,1,0:T(8,128)S(1)} custom-call(s32[1]{0:T(128)} %get-tuple-element.137.offset_ref, f32[5,2,24,384]{3,2,1,0:T(8,128)} %get-tuple-element.138.state_in, f32[2,2,24,384]{3,2,1,0:T(8,128)} %get-tuple-element.139.courant_in), custom_call_target="tpu_custom_call" | custom-call | tf_op jit(solution)/shard_map/cond/branch_11_fun/nested_step_12/pallas_call | solution.py:702
  48.7 0.7 %copy.34 = f32[5,2,24,384]{3,2,1,0:T(8,128)} copy(f32[5,2,24,384]{3,2,1,0:T(8,128)S(1)} %get-tuple-element.146) | data formatting | bytes 737280

commit v2 on v1

--- a/solution.py
+++ b/solution.py
@@ -72,16 +72,19 @@
     at_top = tile == 0
     at_end = at_top | (tile == tiles - 1)
     rim_row = is_nest & at_end
-    row_relay = is_parent & at_end
+    top_relay = tile == (RATIO - 1) * groups
+    row_relay = is_parent & (top_relay | (tile == tiles - 1))
+    rows_tile = pick(at_top, (RATIO - 1) * groups, tiles - 1)
+    rows_to = pick(top_relay, 0, tiles - 1)
     has_left = (section != 0) & (section != 2)
     has_right = (section != 1) & (section != sections - 1)
     low_window = is_parent & (tile >= q - 1) & (tile <= q + 1)
     high_window = is_parent & (tile >= q + groups - 1) & (tile <= q + groups)
     in_window = low_window | high_window
-    window_to = pick(low_window, 0, tiles - 1)
+    window_to = pick(low_window, (RATIO - 1) * groups, tiles - 1)
     window_slot = pick(low_window, tile - q + 1, tile - q - groups + 1)
-    window_first = pick(at_top, q - 1, q + groups - 1)
-    window_count = pick(at_top, 3, 2)
+    window_first = pick(top_relay, q - 1, q + groups - 1)
+    window_count = pick(top_relay, 3, 2)
     under = is_parent & (tile >= q) & (tile <= q + groups)
     third = lax.rem(lax.max(nest, 0), RATIO)
     owner = lax.max(nest, 0) // RATIO
@@ -121,7 +124,7 @@
             barrier, inc=1, device_id=(tile_to, section_to), device_id_type=MESH
         )
 
-    rim_section = pick(section == 0, 2, sections - 1)
+    rim_section = pick(section == 0, sections - 1, 2)
 
     @pl.when(is_parent)
     def _():
@@ -129,25 +132,18 @@
 
         @pl.loop(0, 4)
         def _(d):
-            sender = q + group + d - 1
-
-            @pl.when(sender != tile)
-            def _():
-                greet(sender, section)
+            greet(q + group + d - 1, 1 - section)
 
     @pl.when(row_relay)
     def _():
         @pl.loop(0, RATIO)
         def _(k):
-            greet(tile, 2 + RATIO * section + k)
+            greet(rows_to, 2 + RATIO * section + k)
 
         @pl.loop(0, window_count)
         def _(u):
-            greet(window_first + u, 1 - section)
-
-            @pl.when(window_first + u != tile)
-            def _():
-                greet(window_first + u, section)
+            greet(window_first + u, 0)
+            greet(window_first + u, 1)
 
     for step in NEAR[:2]:
         greet(*near_peer(step))
@@ -250,11 +246,9 @@
             window_rows(FIELDS + d, lambda l: courant.at[d, l])
 
     edge_targets = sum(
-        jnp.where((tile - q + 1 - d >= 0) & (tile - q + 1 - d < groups), RATIO, 0)
-        - jnp.where(tile - q + 1 - d == group, 1, 0)
-        for d in range(4)
+        jnp.where((tile - q + 1 - d >= 0) & (tile - q + 1 - d < groups), RATIO, 0) for d in range(4)
     )
-    window_targets = jnp.where(in_window, 1, 0) + jnp.where(in_window & (window_to != tile), 1, 0)
+    window_targets = jnp.where(in_window, 2, 0)
     relay_targets = (
         sum(jnp.where(relay_tile(group + late) != tile, 1, 0) for late in range(2))
         + jnp.where(is_relay, 1, 0)
@@ -268,12 +262,12 @@
     @pl.when(rim_column)
     def _():
         pl.semaphore_signal(
-            edge_ready, inc=1, device_id=(tile, pick(section == 2, 0, 1)), device_id_type=MESH
+            edge_ready, inc=1, device_id=(tile, pick(section == 2, 1, 0)), device_id_type=MESH
         )
 
     @pl.when(rim_row)
     def _():
-        pl.semaphore_signal(rows_ready.at[third], inc=1, device_id=(tile, owner), device_id_type=MESH)
+        pl.semaphore_signal(rows_ready.at[third], inc=1, device_id=(rows_tile, owner), device_id_type=MESH)
 
     def remote(source, target, send, recv, device):
         return pltpu.make_async_remote_copy(
@@ -281,38 +275,20 @@
             device_id=device, device_id_type=MESH,
         )
 
-    def start(copy):
-        copy.start()
-
-    def wait_send(copy):
-        copy.wait_send()
-
-    def for_windows(act, act_local):
-        @pl.when(in_window)
-        def _():
-            target = window_in.at[window_slot, 1:4]
-            arrived = window_recv.at[window_slot, 0]
-
-            @pl.when(window_to != tile)
-            def _():
-                act(remote(stage, target, window_send.at[0], arrived, (window_to, section)))
-
-            if act_local is not None:
-                @pl.when(window_to == tile)
-                def _():
-                    act_local(pltpu.make_async_copy(stage, target, arrived))
-
-            act(
-                remote(
-                    stage.at[pick(section == 0, 2, 0)],
-                    window_in.at[window_slot, pick(section == 0, 0, 4)],
-                    window_send.at[1], window_recv.at[window_slot, 1], (window_to, 1 - section),
-                )
-            )
-
-    for_windows(start, start)
-
-    def for_edges(act, act_local):
+    def whole_wait(source, semaphore):
+        pltpu.make_async_copy(source, source, semaphore).wait()
+
+    @pl.when(in_window)
+    def _():
+        remote(
+            stage, window_in.at[window_slot, 1:4], window_send, window_recv, (window_to, section)
+        ).start()
+        remote(
+            stage.at[pick(section == 0, 2, 0)], window_in.at[window_slot, pick(section == 0, 0, 4)],
+            window_send, window_recv, (window_to, 1 - section),
+        ).start()
+
+    def for_edges(act):
         @pl.when(is_parent)
         def _():
             @pl.loop(0, 4)
@@ -321,27 +297,16 @@
 
                 @pl.when((aim >= 0) & (aim < groups))
                 def _():
-                    @pl.loop(0, RATIO)
-                    def _(b):
-                        target = aim * RATIO + b
-
-                        @pl.when(target != tile)
-                        def _():
-                            act(
-                                remote(
-                                    strips.at[section], edge_in.at[d], edge_send.at[d, b],
-                                    edge_recv.at[d], (target, section),
-                                )
-                            )
-
-                        if act_local is not None:
-                            @pl.when(target == tile)
-                            def _():
-                                act_local(
-                                    pltpu.make_async_copy(strips.at[section], edge_in.at[d], edge_recv.at[d])
-                                )
-
-    for_edges(start, start)
+                    act(d, aim)
+
+    def send_edges(d, aim):
+        @pl.loop(0, RATIO)
+        def _(b):
+            remote(
+                strips.at[section], edge_in.at[d], edge_send.at[d], edge_recv, (aim * RATIO + b, 1 - section)
+            ).start()
+
+    for_edges(send_edges)
 
     def near_copy(i):
         source, target = (
@@ -354,36 +319,44 @@
             (strips.at[1, 0:8], near_strips.at[1, 24:32]),
             (strips.at[1, 16:24], near_strips.at[1, 32:40]),
         )[i]
-        return remote(source, target, near_send.at[i], near_recv.at[i], near_peer(NEAR[i]))
-
-    def for_near(act, left_exists, right_exists):
-        @pl.when(left_exists)
+        kind = (0, 0, 1, 1, 1, 2, 2, 2)[i]
+        return remote(source, target, near_send.at[kind], near_recv.at[kind], near_peer(NEAR[i]))
+
+    @pl.when(has_left)
+    def _():
+        for i in (2, 3, 4):
+            near_copy(i).start()
+
+    @pl.when(has_right)
+    def _():
+        for i in (5, 6, 7):
+            near_copy(i).start()
+
+    for i in (0, 1):
+        near_copy(i).start()
+
+    def near_wait(semaphores, first_exists, second_exists):
+        @pl.when(first_exists)
         def _():
-            for i in (2, 3, 4):
-                act(near_copy(i))
-
-        @pl.when(right_exists)
+            whole_wait(near_strips.at[0], semaphores.at[1])
+
+        @pl.when(second_exists)
         def _():
-            for i in (5, 6, 7):
-                act(near_copy(i))
-
-        for i in (0, 1):
-            act(near_copy(i))
-
-    for_near(start, has_left, has_right)
+            whole_wait(near_strips.at[1], semaphores.at[2])
+
+        whole_wait(near_slabs, semaphores.at[0])
 
     def spread_copy():
         return remote(spread, spread_in, spread_send, spread_recv, (tile, rim_section))
 
     def rows_copy(k):
         return remote(
-            rows_out.at[k], rows_in, rows_send.at[k], rows_recv, (tile, 2 + RATIO * section + k)
+            rows_out.at[k], rows_in, rows_send, rows_recv, (rows_to, 2 + RATIO * section + k)
         )
 
     @pl.when(is_parent)
     def _():
-        for d in range(4):
-            pltpu.make_async_copy(strips.at[0], edge_in.at[d], edge_recv.at[d]).wait()
+        whole_wait(edge_in, edge_recv)
         shape = (4 * ROWS, LANES)
         value = edge_in[...].reshape(shape)
         speed_y = pltpu.roll(value, LANES - 3 * PAIRS, 1)
@@ -419,11 +392,13 @@
 
     @pl.when(row_relay)
     def _():
-        @pl.loop(0, window_count)
-        def _(u):
-            beside_slot = pick(section == 0, 4, 0)
-            pltpu.make_async_copy(stage, window_in.at[u, 1:4], window_recv.at[u, 0]).wait()
-            pltpu.make_async_copy(stage.at[0], window_in.at[u, beside_slot], window_recv.at[u, 1]).wait()
+        @pl.when(top_relay)
+        def _():
+            whole_wait(window_in.at[:, 0:4], window_recv)
+
+        @pl.when(jnp.logical_not(top_relay))
+        def _():
+            whole_wait(window_in.at[0:2, 0:4], window_recv)
 
         def window(plane):
             return jnp.concatenate([sum(window_in[u, k, plane] for u in range(3)) for k in range(5)], axis=1)
@@ -477,7 +452,7 @@
     strength = pick(is_parent, 0.0, 1.0 / ZONE)
     mixed[0] = jnp.clip(ZONE - depth, 0, ZONE).astype(jnp.float32) * strength
 
-    for_near(lambda copy: copy.wait_recv(), has_right, has_left)
+    near_wait(near_recv, has_right, has_left)
 
     half = iota((8, LANES), 0) < 4
     beside = []
@@ -555,28 +530,21 @@
     ahead = iota((COLS, LANES), 0) - RATIO * iota((COLS, LANES), 1)
     gather = jnp.where((ahead >= 0) & (ahead < RATIO), 1.0, 0.0).astype(jnp.bfloat16)
 
-    def for_relays(f, act, act_local):
+    def send_means(f):
         @pl.loop(0, 2)
         def _(late):
             target = relay_tile(group + late)
 
             @pl.when(target != tile)
             def _():
-                act(
-                    remote(
-                        means.at[f], relay_in.at[f, late, inner], relay_send.at[f, late],
-                        relay_recv.at[f, late, inner], (target, section),
-                    )
-                )
-
-            if act_local is not None:
-                @pl.when(target == tile)
-                def _():
-                    act_local(
-                        pltpu.make_async_copy(
-                            means.at[f], relay_in.at[f, late, inner], relay_recv.at[f, late, inner]
-                        )
-                    )
+                remote(
+                    means.at[f], relay_in.at[f, late, inner], relay_send.at[late], relay_recv.at[f],
+                    (target, section),
+                ).start()
+
+            @pl.when(target == tile)
+            def _():
+                pltpu.make_async_copy(means.at[f], relay_in.at[f, late, inner], relay_recv.at[f]).start()
 
     steps = pick(is_parent, 1, RATIO)
 
@@ -617,11 +585,11 @@
             ]
             block = dot_ones(jnp.concatenate(sums, axis=1), gather) * (1.0 / (RATIO * RATIO))
             means[f] = block.reshape(LEVELS, COARSE, LANES)
-            for_relays(f, start, start)
+            send_means(f)
 
     def mean_copy(f):
         return remote(
-            relay_out.at[f], mean_in.at[f, third], mean_send.at[f], mean_recv.at[f, third],
+            relay_out.at[f], mean_in.at[f, third], mean_send, mean_recv.at[f],
             (q + task, owner),
         )
 
@@ -629,15 +597,16 @@
     def _():
         @pl.loop(0, FIELDS)
         def _(f):
-            @pl.loop(0, 2)
-            def _(late):
-                @pl.when(relay_source(late))
-                def _():
-                    @pl.loop(0, RATIO)
-                    def _(b):
-                        pltpu.make_async_copy(
-                            means.at[f], relay_in.at[f, late, b], relay_recv.at[f, late, b]
-                        ).wait()
+            full = (task >= 1) & (task < groups)
+
+            @pl.when(full)
+            def _():
+                whole_wait(relay_in.at[f], relay_recv.at[f])
+
+            @pl.when(jnp.logical_not(full))
+            def _():
+                whole_wait(relay_in.at[f, 0], relay_recv.at[f])
+
             for l in range(LEVELS):
                 lined = jnp.concatenate(
                     [relay_in[f, late, b, l] for late in (1, 0) for b in range(RATIO)], axis=0
@@ -652,15 +621,18 @@
 
         @pl.loop(0, FIELDS)
         def _(f):
-            for c in range(RATIO):
-                pltpu.make_async_copy(relay_out.at[f], mean_in.at[f, c], mean_recv.at[f, c]).wait()
+            whole_wait(mean_in.at[f], mean_recv.at[f])
             for l in range(LEVELS):
                 fed = jnp.concatenate([mean_in[f, c, l] for c in range(RATIO)], axis=1)
                 out[f, l] = jnp.where(covered, fed, out[f, l])
 
-    for_near(wait_send, has_left, has_right)
-    for_windows(wait_send, None)
-    for_edges(wait_send, None)
+    near_wait(near_send, has_left, has_right)
+
+    @pl.when(in_window)
+    def _():
+        whole_wait(window_in.at[0, 0:4], window_send)
+
+    for_edges(lambda d, aim: whole_wait(edge_in.at[0:RATIO], edge_send.at[d]))
 
     @pl.when(is_parent)
     def _():
@@ -668,21 +640,19 @@
 
     @pl.when(row_relay)
     def _():
-        @pl.loop(0, RATIO)
-        def _(k):
-            rows_copy(k).wait_send()
+        whole_wait(rows_out, rows_send)
 
     @pl.when(is_nest)
     def _():
-        @pl.loop(0, FIELDS)
-        def _(f):
-            for_relays(f, wait_send, None)
+        @pl.loop(0, 2)
+        def _(late):
+            @pl.when(relay_tile(group + late) != tile)
+            def _():
+                whole_wait(means, relay_send.at[late])
 
     @pl.when(is_relay)
     def _():
-        @pl.loop(0, FIELDS)
-        def _(f):
-            mean_copy(f).wait_send()
+        whole_wait(relay_out, mean_send)
 
 
 def solution(mesh):
@@ -699,6 +669,7 @@
         def copies(*shape):
             return pltpu.SemaphoreType.DMA(shape)
 
+        one = pltpu.SemaphoreType.DMA
         return pl.pallas_call(
             functools.partial(kernel, q, tiles, sections),
             out_shape=jax.ShapeDtypeStruct(state.shape, state.dtype),
@@ -729,10 +700,9 @@
                 space(FIELDS, 2, RATIO, LEVELS, COARSE, LANES),
                 space(FIELDS, LEVELS, ROWS, LANES),
                 space(FIELDS, RATIO, LEVELS, ROWS, LANES),
-                copies(2), copies(8), copies(8), copies(4, RATIO), copies(4), copies(2), copies(3, 2),
-                pltpu.SemaphoreType.DMA, pltpu.SemaphoreType.DMA, copies(RATIO), pltpu.SemaphoreType.DMA,
-                pltpu.SemaphoreType.REGULAR, pltpu.SemaphoreType.REGULAR((RATIO,)),
-                copies(FIELDS, 2), copies(FIELDS, 2, RATIO), copies(FIELDS), copies(FIELDS, RATIO),
+                copies(2), copies(3), copies(3), copies(4), one, one, one,
+                one, one, one, one, pltpu.SemaphoreType.REGULAR, pltpu.SemaphoreType.REGULAR((RATIO,)),
+                copies(2), copies(FIELDS), one, copies(FIELDS),
             ],
             compiler_params=pltpu.CompilerParams(collective_id=q, has_side_effects=True),
             name=f"nested_step_{q}",

time: 49.6 us -> 51.1 us (1.030)
  the two profiles are of different devices: /device:TPU:34 before, /device:TPU:82 now
where the time goes in v2:
time: 51.1 us; the launch traced here: 50.9 us
  Pallas kernels  49 us (96%)
  local copies, waits for them, and re-layouts  0.74 us (1%)
  between operations  0.69 us (1%)
  loops' own time  0.54 us (1%)
    pallas_call x1, Pallas kernels, call(): pl.pallas_call(functools.partial(kernel, q, tiles, sections), out_shape=j...  49 us

profile of v2, /device:TPU:82, one launch (start us, length us, event | category | flops | bytes accessed | tf_op | source)
XLA Modules:
  0.0 50.9 jit_solution(4011426956996105567)
XLA Ops:
  0.7 49.5 %conditional.1 = (f32[5,2,24,384]{3,2,1,0:T(8,128)S(1)}) conditional(s32[]{:T(128)} %clamp.3, (s32[1]{0:T(128)}, f32[5,2,24,384]{3,2,1,0:T(8,128)}, f32[2,2,24,384]{3,2,1,0:T(8,128)}) %tuple.47, (s32[1]{0:T(128)}, f32[5,2,24,384]{3,2,1,0:T(8,128)}, f32[2,2,24,384]{3,2,1,0:T(8,128)}) %tuple.47, (s32[1]{0:T(128)}, ...), branch_computations={%region_0.1_spmd, %region_1.2_spmd, %region_2.3_spmd, %region_3.4_... | conditional | bytes 8 | solution.py:714
  0.9 49.0 %nested_step_11.1 = f32[5,2,24,384]{3,2,1,0:T(8,128)S(1)} custom-call(s32[1]{0:T(128)} %get-tuple-element.134.offset_ref, f32[5,2,24,384]{3,2,1,0:T(8,128)} %get-tuple-element.135.state_in, f32[2,2,24,384]{3,2,1,0:T(8,128)} %get-tuple-element.136.courant_in), custom_call_target="tpu_custom_call" | custom-call | tf_op jit(solution)/shard_map/cond/branch_10_fun/nested_step_11/pallas_call | solution.py:673
  50.2 0.7 %copy.34 = f32[5,2,24,384]{3,2,1,0:T(8,128)} copy(f32[5,2,24,384]{3,2,1,0:T(8,128)S(1)} %get-tuple-element.146) | data formatting | bytes 737280

commit v3 on v2

--- a/solution.py
+++ b/solution.py
@@ -73,15 +73,15 @@
     at_end = at_top | (tile == tiles - 1)
     rim_row = is_nest & at_end
     top_relay = tile == (RATIO - 1) * groups
-    row_relay = is_parent & (top_relay | (tile == tiles - 1))
-    rows_tile = pick(at_top, (RATIO - 1) * groups, tiles - 1)
+    row_relay = is_parent & (top_relay | (tile == groups - 1))
+    rows_tile = pick(at_top, (RATIO - 1) * groups, groups - 1)
     rows_to = pick(top_relay, 0, tiles - 1)
     has_left = (section != 0) & (section != 2)
     has_right = (section != 1) & (section != sections - 1)
     low_window = is_parent & (tile >= q - 1) & (tile <= q + 1)
     high_window = is_parent & (tile >= q + groups - 1) & (tile <= q + groups)
     in_window = low_window | high_window
-    window_to = pick(low_window, (RATIO - 1) * groups, tiles - 1)
+    window_to = pick(low_window, (RATIO - 1) * groups, groups - 1)
     window_slot = pick(low_window, tile - q + 1, tile - q - groups + 1)
     window_first = pick(top_relay, q - 1, q + groups - 1)
     window_count = pick(top_relay, 3, 2)
@@ -89,13 +89,17 @@
     third = lax.rem(lax.max(nest, 0), RATIO)
     owner = lax.max(nest, 0) // RATIO
 
-    def relay_tile(a):
-        return lax.min(a, groups - 1) * RATIO // groups * groups + lax.rem(q + a, groups)
+    middle = (section == 4) | (section == 5)
+
+    def relay_tile(a, middle):
+        plane = lax.min(a, groups - 1) * RATIO // groups
+        plane = pick(middle & (a == 0), 1, pick(middle & (a == groups), 0, plane))
+        return plane * groups + lax.rem(q + a, groups)
 
     turn = lax.rem(tile - q + tiles, groups)
-    wrapped = (turn == 0) & (tile // groups == RATIO - 1)
+    wrapped = (turn == 0) & (tile // groups == pick(middle, 0, RATIO - 1))
     task = pick(wrapped, groups, turn)
-    is_relay = is_nest & (relay_tile(task) == tile)
+    is_relay = is_nest & (relay_tile(task, middle) == tile)
 
     def near_peer(step):
         return lax.rem(tile + step[0] + tiles, tiles), section + step[1]
@@ -179,7 +183,8 @@
     def _():
         @pl.loop(0, RATIO)
         def _(third):
-            greet(relay_tile(tile - q), 2 + RATIO * section + third)
+            mate = 2 + RATIO * section + third
+            greet(relay_tile(tile - q, (mate == 4) | (mate == 5)), mate)
 
     @pl.loop(0, PAIRS)
     def _(pair):
@@ -250,7 +255,7 @@
     )
     window_targets = jnp.where(in_window, 2, 0)
     relay_targets = (
-        sum(jnp.where(relay_tile(group + late) != tile, 1, 0) for late in range(2))
+        sum(jnp.where(relay_tile(group + late, middle) != tile, 1, 0) for late in range(2))
         + jnp.where(is_relay, 1, 0)
         + jnp.where(rim_column, 1, 0)
         + jnp.where(rim_row, 1, 0)
@@ -387,9 +392,6 @@
         )
         spread[0] = rows[:, :LANES]
         spread[1] = rows[:, LANES:]
-        pl.semaphore_wait(edge_ready, 1)
-        spread_copy().start()
-
     @pl.when(row_relay)
     def _():
         @pl.when(top_relay)
@@ -438,10 +440,18 @@
             lanes = pl.ds(pl.multiple_of(LANES * k, LANES), LANES)
             rows_out[:, :, :, lanes] = dot_ones(stacked, widen).reshape(RATIO, FIELDS, 8, LANES)
 
+    @pl.when(row_relay)
+    def _():
         @pl.loop(0, RATIO)
         def _(k):
             pl.semaphore_wait(rows_ready.at[k], 1)
             rows_copy(k).start()
+
+    @pl.when(is_parent)
+    def _():
+        pl.semaphore_wait(edge_ready, 1)
+        spread_copy().start()
+
     row = iota((TALL, WIDE), 0)
     col = iota((TALL, WIDE), 1)
     row = tile * ROWS + jnp.where(row < 28, row, row - TALL)
@@ -533,7 +543,7 @@
     def send_means(f):
         @pl.loop(0, 2)
         def _(late):
-            target = relay_tile(group + late)
+            target = relay_tile(group + late, middle)
 
             @pl.when(target != tile)
             def _():
@@ -646,7 +656,7 @@
     def _():
         @pl.loop(0, 2)
         def _(late):
-            @pl.when(relay_tile(group + late) != tile)
+            @pl.when(relay_tile(group + late, middle) != tile)
             def _():
                 whole_wait(means, relay_send.at[late])
 

time: 51.1 us -> 44.6 us (0.87)
  the two profiles are of different devices: /device:TPU:82 before, /device:TPU:50 now
where the time goes in v3:
time: 44.6 us; the launch traced here: 44.4 us
  Pallas kernels  42.5 us (95%)
  local copies, waits for them, and re-layouts  0.74 us (2%)
  between operations  0.69 us (2%)
  loops' own time  0.54 us (1%)
    pallas_call x1, Pallas kernels, call(): pl.pallas_call(functools.partial(kernel, q, tiles, sections), out_shape=j...  42.5 us

profile of v3, /device:TPU:50, one launch (start us, length us, event | category | flops | bytes accessed | tf_op | source)
XLA Modules:
  0.0 44.4 jit_solution(4176581276424030626)
XLA Ops:
  0.7 43.0 %conditional.1 = (f32[5,2,24,384]{3,2,1,0:T(8,128)S(1)}) conditional(s32[]{:T(128)} %clamp.3, (s32[1]{0:T(128)}, f32[5,2,24,384]{3,2,1,0:T(8,128)}, f32[2,2,24,384]{3,2,1,0:T(8,128)}) %tuple.47, (s32[1]{0:T(128)}, f32[5,2,24,384]{3,2,1,0:T(8,128)}, f32[2,2,24,384]{3,2,1,0:T(8,128)}) %tuple.47, (s32[1]{0:T(128)}, ...), branch_computations={%region_0.1_spmd, %region_1.2_spmd, %region_2.3_spmd, %region_3.4_... | conditional | bytes 8 | solution.py:724
  1.0 42.5 %nested_step_14.1 = f32[5,2,24,384]{3,2,1,0:T(8,128)S(1)} custom-call(s32[1]{0:T(128)} %get-tuple-element.143.offset_ref, f32[5,2,24,384]{3,2,1,0:T(8,128)} %get-tuple-element.144.state_in, f32[2,2,24,384]{3,2,1,0:T(8,128)} %get-tuple-element.145.courant_in), custom_call_target="tpu_custom_call" | custom-call | tf_op jit(solution)/shard_map/cond/branch_13_fun/nested_step_14/pallas_call | solution.py:683
  43.7 0.7 %copy.34 = f32[5,2,24,384]{3,2,1,0:T(8,128)} copy(f32[5,2,24,384]{3,2,1,0:T(8,128)S(1)} %get-tuple-element.146) | data formatting | bytes 737280
